TPU v7x, 32 devices: a whole 2x2x4 slice. The times are simulated.
32 devices in a mesh: frame: 8 (over z, y), height: 4 (over x, core).
Axes of the slice: x: 2, y: 2, z: 4, core: 2. Of those that a mesh axis runs over, the one named last changes fastest.
Arguments:
- latents: bfloat16 [8, 24, 64, 1152], P('frame', 'height'), may hold values from -30 to 30
- qkv_weight: bfloat16 [2, 1152, 1728], replicated, as said below
- out_weight: bfloat16 [2, 576, 1152], replicated, may hold values from -0.25 to 0.25
Outputs:
- result: bfloat16 [8, 24, 64, 1152], P('frame', 'height')
Inputs may be any that keep to these rules, and one draw needn't show every extreme that they name: `qkv_weight`: entries lie within -0.2 to 0.2.
All inputs are finite; a program needn't handle non-finite values.
Results may differ from a plain program's by a relative error of at most 0.0095.
Values may be sent and summed in bfloat16 or wider, within the bound.
No kernel may reach another device: no remote copies, remote signals or barrier semaphores. Data moves between devices by JAX's collectives and lax.ppermute only.
A program may use at most 64 MiB of HBM per device.

v0:
```python
import jax
import jax.numpy as jnp
from jax import lax
from jax.sharding import PartitionSpec as P

HEAD_DIM = 72


def layer_norm(values):
    values = values.astype(jnp.float32)
    center = values - jnp.mean(values, axis=-1, keepdims=True)
    spread = jnp.mean(center * center, axis=-1, keepdims=True)
    return (center * lax.rsqrt(spread + 1e-06)).astype(jnp.bfloat16)


def project(tokens, weight):
    normed = layer_norm(tokens)
    flattened = normed.reshape(-1, normed.shape[-1])
    joined = jnp.dot(flattened, weight, preferred_element_type=jnp.float32)
    return joined.astype(jnp.bfloat16).reshape(tokens.shape[:-1] + (weight.shape[1],))


def attend(joined):
    length, batches = (joined.shape[0], joined.shape[1])
    inner_width = joined.shape[2] // 3
    head_count = inner_width // HEAD_DIM
    query_rows = joined[:, :, :inner_width].reshape(length, batches, head_count, HEAD_DIM)
    key_rows = joined[:, :, inner_width : 2 * inner_width].reshape(
        length, batches, head_count, HEAD_DIM
    )
    value_rows = joined[:, :, 2 * inner_width :].reshape(length, batches, head_count, HEAD_DIM)
    scores = jnp.einsum(
        "lbnd,mbnd->bnlm", query_rows, key_rows, preferred_element_type=jnp.float32
    ) * HEAD_DIM ** (-0.5)
    scores = scores - jnp.max(scores, axis=-1, keepdims=True)
    exponent = jnp.exp(scores)
    weights = (exponent / jnp.sum(exponent, axis=-1, keepdims=True)).astype(jnp.bfloat16)
    mixture = jnp.einsum("bnlm,mbnd->lbnd", weights, value_rows, preferred_element_type=jnp.float32)
    return mixture.reshape(length, batches, inner_width).astype(jnp.bfloat16)


def residual(tokens, mixture, weight):
    update = jnp.dot(
        mixture.reshape(-1, mixture.shape[-1]), weight, preferred_element_type=jnp.float32
    )
    return (tokens.astype(jnp.float32) + update.reshape(tokens.shape)).astype(jnp.bfloat16)


def frames_block(joined):
    length, single, places, triple = joined.shape
    mixture = attend(joined.reshape(length, single * places, triple))
    return mixture.reshape(length, single, places, triple // 3)


def per_device(latents, qkv_weight, out_weight):
    frames_dev, rows_dev, columns, feature_width = latents.shape
    frame_count = lax.axis_size("frame")
    rows_attend = jax.vmap(attend)
    rows_att = rows_attend(
        project(
            lax.all_to_all(latents, "height", split_axis=2, concat_axis=1, tiled=True),
            qkv_weight[0],
        )
    )
    rows_att = lax.all_to_all(rows_att, "height", split_axis=1, concat_axis=2, tiled=True)
    middle = residual(latents, rows_att, out_weight[0])
    places_dev = rows_dev * columns // frame_count
    grouped = middle.reshape(frames_dev, frame_count, places_dev, feature_width)
    frames_att = frames_block(
        project(
            lax.all_to_all(grouped, "frame", split_axis=1, concat_axis=0, tiled=True), qkv_weight[1]
        )
    )
    frames_att = lax.all_to_all(frames_att, "frame", split_axis=0, concat_axis=1, tiled=True)
    frames_att = frames_att.reshape(frames_dev, rows_dev, columns, frames_att.shape[-1])
    return residual(middle, frames_att, out_weight[1])


def solution(mesh):
    return jax.shard_map(
        per_device,
        mesh=mesh,
        in_specs=(P("frame", "height", None, None), P(), P()),
        out_specs=P("frame", "height", None, None),
        check_vma=False,
    )
```

profile of v0, /device:TPU:0, one launch (start us, length us, event | category | flops | bytes accessed | tf_op | source)
XLA Modules:
  0.0 113.4 jit_solution(6258203247795227640)
XLA Ops:
  0.0 1.7 %copy.33 = bf16[1,6,64,1152]{3,1,0,2:T(8,128)(2,1)S(1)} copy(bf16[1,6,64,1152]{3,2,1,0:T(8,128)(2,1)} %param.3) | data formatting | bytes 1769472 | tf_op args[0]
  1.7 20.1 %all_to_all.42 = bf16[1,6,64,1152]{3,1,0,2:T(8,128)(2,1)S(1)} all-to-all(bf16[1,6,64,1152]{3,1,0,2:T(8,128)(2,1)S(1)} %copy.33), channel_id=1, replica_groups=mesh['frame'=8,'height'=4] {'height'}, dimensions={2} | all-to-all | bytes 1769472 | tf_op jit(solution)/shard_map/all_to_all | solution.py:61
  21.9 0.2 fusion.24
  22.2 0.4 fusion.27
  22.5 0.3 fusion.28
  22.9 2.4 %fusion.12 = bf16[384,1728]{0,1:T(8,128)(2,1)S(1)} fusion(bf16[384,1152]{1,0:T(8,128)(2,1)S(1)} %bitcast.98, bf16[2,1152,1728]{1,2,0:T(8,128)(2,1)S(1)} %copy-done.5), kind=kOutput, calls=%fused_computation.14 | convolution fusion | flops 1529487360 | bytes 6193152 | tf_op jit(solution)/shard_map/dot_general | solution.py:19
  25.3 1.8 %copy.36 = bf16[384,1728]{1,0:T(8,128)(2,1)S(1)} copy(bf16[384,1728]{0,1:T(8,128)(2,1)S(1)} %fusion.12) | data formatting | bytes 2654208 | tf_op jit(solution)/shard_map/convert_element_type | solution.py:20
  27.1 0.3 fusion.68
  27.3 0.8 reshape.264
  28.1 0.8 reshape.265
  28.9 1.7 %reshape.263 = bf16[24,16,8,72]{3,2,1,0:T(8,128)(2,1)} reshape(bf16[1,24,16,576]{3,2,1,0:T(8,128)(2,1)S(1)} %get-tuple-element.8) | data formatting | bytes 884736 | tf_op jit(solution)/shard_map/reshape.7
  30.6 2.6 %fusion.69 = (f32[16,8,24]{2,1,0:T(8,128)S(1)}, f32[16,8,24,24]{2,3,1,0:T(8,128)}) fusion(bf16[24,16,8,72]{3,2,1,0:T(8,128)(2,1)S(1)} %reshape.265, bf16[24,16,8,72]{3,2,1,0:T(8,128)(2,1)S(1)} %reshape.264), kind=kOutput, calls=%fused_computation.65 | convolution fusion | flops 10838039 | bytes 1191936 | tf_op jit(solution)/shard_map/vmap()/sub | solution.py:35
  33.2 2.1 %fusion.37 = bf16[1,24,16,8,72]{4,1,3,2,0:T(8,128)(2,1)S(1)} fusion(f32[16,8,24,24]{2,3,1,0:T(8,128)} %get-tuple-element.12, bf16[24,16,8,72]{3,2,1,0:T(8,128)(2,1)S(1)} %copy-done.3, f32[16,8,24]{2,1,0:T(8,128)S(1)} %get-tuple-element.11), kind=kOutput, calls=%fused_computation.45 | convolution fusion | flops 10985472 | bytes 1191936 | tf_op jit(solution)/shard_map/vmap(bnlm,mbnd->lbnd)/dot_general | solution.py:38
  35.4 0.2 copy.41
  35.5 0.6 convert_element_type.136
  36.1 10.9 %all_to_all.43 = bf16[1,24,16,576]{3,2,0,1:T(8,128)(2,1)S(1)} all-to-all(bf16[1,24,16,576]{3,2,0,1:T(8,128)(2,1)S(1)} %bitcast.93), channel_id=1, replica_groups=mesh['frame'=8,'height'=4] {'height'}, dimensions={1} | all-to-all | bytes 884736 | tf_op jit(solution)/shard_map/all_to_all | solution.py:65
  47.0 2.3 %fusion.10 = bf16[1,6,64,1152]{3,2,1,0:T(8,128)(2,1)S(1)} fusion(bf16[6,64,576]{2,1,0:T(8,128)(2,1)S(1)} %bitcast.100, bf16[1,6,64,1152]{3,2,1,0:T(8,128)(2,1)S(1)} %copy-done.2, bf16[2,576,1152]{2,1,0:T(8,128)(2,1)} %param.5), kind=kOutput, calls=%fused_computation.12 | convolution fusion | flops 510935040 | bytes 3538944 | tf_op jit(solution)/shard_map/dot_general | solution.py:43
  49.3 28.1 %all_to_all.44 = bf16[1,8,48,1152]{3,2,0,1:T(8,128)(2,1)S(1)} all-to-all(bf16[1,8,48,1152]{3,2,0,1:T(8,128)(2,1)S(1)} %bitcast.96), channel_id=1, replica_groups=mesh['frame'=8,'height'=4] {'frame'}, dimensions={1} | all-to-all | bytes 1769472 | tf_op jit(solution)/shard_map/all_to_all | solution.py:71
  77.5 0.2 convert_reduce_fusion
  77.7 0.4 fusion.22
  78.1 0.3 fusion.19
  78.4 4.5 %fusion.15 = bf16[384,1728]{0,1:T(8,128)(2,1)S(1)} fusion(bf16[384,1152]{1,0:T(8,128)(2,1)S(1)} %bitcast.97, bf16[2,1152,1728]{1,2,0:T(8,128)(2,1)} %param.4), kind=kOutput, calls=%fused_computation.15 | convolution fusion | flops 1529487360 | bytes 6193152 | tf_op jit(solution)/shard_map/dot_general | solution.py:19
  82.8 1.8 %copy.45 = bf16[384,1728]{1,0:T(8,128)(2,1)S(1)} copy(bf16[384,1728]{0,1:T(8,128)(2,1)S(1)} %fusion.15) | data formatting | bytes 2654208 | tf_op jit(solution)/shard_map/convert_element_type | solution.py:20
  84.6 0.3 fusion.67
  84.9 0.8 reshape.269
  85.7 0.8 reshape.270
  86.5 1.7 %reshape.268 = bf16[8,48,8,72]{3,2,1,0:T(8,128)(2,1)} reshape(bf16[8,48,576]{2,1,0:T(8,128)(2,1)S(1)} %get-tuple-element.5) | data formatting | bytes 884736 | tf_op jit(solution)/shard_map/reshape | solution.py:31
  88.1 2.8 %fusion.74 = (f32[48,8,8]{2,1,0:T(8,128)S(1)}, f32[48,8,8,8]{2,3,1,0:T(8,128)}) fusion(bf16[8,48,8,72]{3,2,1,0:T(8,128)(2,1)S(1)} %reshape.270, bf16[8,48,8,72]{3,2,1,0:T(8,128)(2,1)S(1)} %reshape.269), kind=kOutput, calls=%fused_computation.66 | convolution fusion | flops 3612679 | bytes 995328 | tf_op jit(solution)/shard_map/sub | solution.py:35
  90.9 2.2 %fusion.38 = bf16[8,48,8,72]{3,0,2,1:T(8,128)(2,1)S(1)} fusion(f32[48,8,8,8]{2,3,1,0:T(8,128)} %get-tuple-element.14, bf16[8,48,8,72]{3,2,1,0:T(8,128)(2,1)S(1)} %copy-done.4, f32[48,8,8]{2,1,0:T(8,128)S(1)} %get-tuple-element.13), kind=kOutput, calls=%fused_computation.46 | convolution fusion | flops 3809280 | bytes 995328 | tf_op jit(solution)/shard_map/bnlm,mbnd->lbnd/dot_general | solution.py:38
  93.2 0.6 convert_element_type.147
  93.8 16.4 %all_to_all.45 = bf16[8,1,48,576]{3,2,1,0:T(8,128)(2,1)S(1)} all-to-all(bf16[8,1,48,576]{3,2,1,0:T(8,128)(2,1)S(1)} %bitcast.95), channel_id=1, replica_groups=mesh['frame'=8,'height'=4] {'frame'}, dimensions={0} | all-to-all | bytes 884736 | tf_op jit(solution)/shard_map/all_to_all | solution.py:74
  110.2 3.2 %fusion.11 = bf16[1,6,64,1152]{3,2,1,0:T(8,128)(2,1)} fusion(bf16[6,64,576]{2,1,0:T(8,128)(2,1)S(1)} %bitcast.99, bf16[1,6,64,1152]{3,2,1,0:T(8,128)(2,1)S(1)} %copy-done.1, bf16[2,576,1152]{2,1,0:T(8,128)(2,1)} %param.5), kind=kOutput, calls=%fused_computation.13 | convolution fusion | flops 510935040 | bytes 3538944 | tf_op jit(solution)/shard_map/dot_general | solution.py:43
  (20 shorter events, 0.4 us)
Async XLA Ops:
  1.7 21.2 %copy-start.5 = (bf16[2,1152,1728]{1,2,0:T(8,128)(2,1)S(1)}, bf16[2,1152,1728]{1,2,0:T(8,128)(2,1)}, u32[]{:S(2)}) copy-start(bf16[2,1152,1728]{1,2,0:T(8,128)(2,1)} %param.4) | copy-start | bytes 23887876
  30.6 2.6 %copy-start.3 = (bf16[24,16,8,72]{3,2,1,0:T(8,128)(2,1)S(1)}, bf16[24,16,8,72]{3,2,1,0:T(8,128)(2,1)}, u32[]{:S(2)}) copy-start(bf16[24,16,8,72]{3,2,1,0:T(8,128)(2,1)} %reshape.263) | copy-start | bytes 1327108
  35.5 11.5 %copy-start.2 = (bf16[1,6,64,1152]{3,2,1,0:T(8,128)(2,1)S(1)}, bf16[1,6,64,1152]{3,2,1,0:T(8,128)(2,1)}, u32[]{:S(2)}) copy-start(bf16[1,6,64,1152]{3,2,1,0:T(8,128)(2,1)} %param.3) | copy-start | bytes 2654212
  49.3 28.7 %copy-start = (bf16[1,6,64,1152]{3,2,1,0:T(8,128)(2,1)}, bf16[1,6,64,1152]{3,2,1,0:T(8,128)(2,1)S(1)}, u32[]{:S(2)}) copy-start(bf16[1,6,64,1152]{3,2,1,0:T(8,128)(2,1)S(1)} %fusion.10) | copy-start | bytes 2654212
  88.1 2.8 %copy-start.4 = (bf16[8,48,8,72]{3,2,1,0:T(8,128)(2,1)S(1)}, bf16[8,48,8,72]{3,2,1,0:T(8,128)(2,1)}, u32[]{:S(2)}) copy-start(bf16[8,48,8,72]{3,2,1,0:T(8,128)(2,1)} %reshape.268) | copy-start | bytes 1327108
  93.1 17.1 %copy-start.1 = (bf16[1,6,64,1152]{3,2,1,0:T(8,128)(2,1)S(1)}, bf16[1,6,64,1152]{3,2,1,0:T(8,128)(2,1)}, u32[]{:S(2)}) copy-start(bf16[1,6,64,1152]{3,2,1,0:T(8,128)(2,1)} %copy-done) | copy-start | bytes 2654212
where the time goes:
time: 114 us; the launch traced here: 113 us
  blocking collectives  75.5 us (66%)
  matrix products  22 us (19%)
  local copies, waits for them, and re-layouts  13.9 us (12%)
  other arithmetic  1.71 us (2%)
    all_to_all x1, blocking collectives, per_device(): lax.all_to_all(grouped, 'frame', split_axis=1, concat_axis=0, tiled=True)  28.1 us
    all_to_all x1, blocking collectives, per_device(): lax.all_to_all(latents, 'height', split_axis=2, concat_axis=1, tiled=True)  20.1 us
    all_to_all x1, blocking collectives, per_device(): lax.all_to_all(frames_att, 'frame', split_axis=0, concat_axis=1, tiled=True)  16.4 us
    all_to_all x1, blocking collectives, per_device(): lax.all_to_all(rows_att, 'height', split_axis=1, concat_axis=2, tiled=True)  10.9 us
    dot_general x2, matrix products, project(): joined = jnp.dot(flattened, weight, preferred_element_type=jnp.float32)  6.84 us
    dot_general x2, matrix products, residual(): jnp.dot(mixture.reshape(-1, mixture.shape[-1]), weight, preferred_element...  5.45 us
    sub x2, matrix products, attend(): scores = scores - jnp.max(scores, axis=-1, keepdims=True)  5.41 us
    dot_general x2, matrix products, attend(): jnp.einsum('bnlm,mbnd->lbnd', weights, value_rows, preferred_element_type...  4.31 us

commit v1 on v0

--- a/solution.py
+++ b/solution.py
@@ -71,7 +71,9 @@
             lax.all_to_all(grouped, "frame", split_axis=1, concat_axis=0, tiled=True), qkv_weight[1]
         )
     )
-    frames_att = lax.all_to_all(frames_att, "frame", split_axis=0, concat_axis=1, tiled=True)
+    shards = jnp.split(frames_att, lax.axis_size("frame"), axis=0)
+    got = lax.all_to_all(jnp.stack(shards), "frame", 0, 0)
+    frames_att = jnp.concatenate(got, axis=1)
     frames_att = frames_att.reshape(frames_dev, rows_dev, columns, frames_att.shape[-1])
     return residual(middle, frames_att, out_weight[1])
 

time: 114 us -> 119 us (1.044)
  local copies, waits for them, and re-layouts: 13.9 us -> 18.9 us
    split x0 -> x1, local copies, waits for them, and re-layouts: none -> 4.56 us  [per_device(): shards = jnp.split(frames_att, lax.axis_size('frame'), axis=0)]
    another operation x3 -> x12, local copies, waits for them, and re-layouts: 3.23 us -> 4.27 us
where the time goes in v1:
time: 119 us; the launch traced here: 118 us
  blocking collectives  75.5 us (63%)
  matrix products  22 us (18%)
  local copies, waits for them, and re-layouts  18.9 us (16%)
  other arithmetic  1.71 us (1%)
    all_to_all x1, blocking collectives, per_device(): lax.all_to_all(grouped, 'frame', split_axis=1, concat_axis=0, tiled=True)  28.1 us
    all_to_all x1, blocking collectives, per_device(): lax.all_to_all(latents, 'height', split_axis=2, concat_axis=1, tiled=True)  20.1 us
    all_to_all x1, blocking collectives, per_device(): got = lax.all_to_all(jnp.stack(shards), 'frame', 0, 0)  16.4 us
    all_to_all x1, blocking collectives, per_device(): lax.all_to_all(rows_att, 'height', split_axis=1, concat_axis=2, tiled=True)  10.9 us
    dot_general x2, matrix products, project(): joined = jnp.dot(flattened, weight, preferred_element_type=jnp.float32)  6.84 us
    dot_general x2, matrix products, residual(): jnp.dot(mixture.reshape(-1, mixture.shape[-1]), weight, preferred_element...  5.45 us
    sub x2, matrix products, attend(): scores = scores - jnp.max(scores, axis=-1, keepdims=True)  5.41 us
    split x1, local copies, waits for them, and re-layouts, per_device(): shards = jnp.split(frames_att, lax.axis_size('frame'), axis=0)  4.56 us

profile of v1, /device:TPU:0, one launch (start us, length us, event | category | flops | bytes accessed | tf_op | source)
XLA Modules:
  0.0 118.4 jit_solution(10630902428151552163)
XLA Ops:
  0.0 1.7 %copy.31 = bf16[1,6,64,1152]{3,1,0,2:T(8,128)(2,1)S(1)} copy(bf16[1,6,64,1152]{3,2,1,0:T(8,128)(2,1)} %param.3) | data formatting | bytes 1769472 | tf_op args[0]
  1.7 20.1 %all_to_all.38 = bf16[1,6,64,1152]{3,1,0,2:T(8,128)(2,1)S(1)} all-to-all(bf16[1,6,64,1152]{3,1,0,2:T(8,128)(2,1)S(1)} %copy.31), channel_id=1, replica_groups=mesh['frame'=8,'height'=4] {'height'}, dimensions={2} | all-to-all | bytes 1769472 | tf_op jit(solution)/shard_map/all_to_all | solution.py:61
  21.9 0.2 fusion.24
  22.2 0.4 fusion.27
  22.5 0.3 fusion.28
  22.9 2.4 %fusion.12 = bf16[384,1728]{0,1:T(8,128)(2,1)S(1)} fusion(bf16[384,1152]{1,0:T(8,128)(2,1)S(1)} %bitcast.94, bf16[2,1152,1728]{1,2,0:T(8,128)(2,1)S(1)} %copy-done.5), kind=kOutput, calls=%fused_computation.14 | convolution fusion | flops 1529487360 | bytes 6193152 | tf_op jit(solution)/shard_map/dot_general | solution.py:19
  25.3 1.8 %copy.34 = bf16[384,1728]{1,0:T(8,128)(2,1)S(1)} copy(bf16[384,1728]{0,1:T(8,128)(2,1)S(1)} %fusion.12) | data formatting | bytes 2654208 | tf_op jit(solution)/shard_map/convert_element_type | solution.py:20
  27.1 0.3 fusion.68
  27.3 0.8 reshape.282
  28.1 0.8 reshape.283
  28.9 1.7 %reshape.281 = bf16[24,16,8,72]{3,2,1,0:T(8,128)(2,1)} reshape(bf16[1,24,16,576]{3,2,1,0:T(8,128)(2,1)S(1)} %get-tuple-element.16) | data formatting | bytes 884736 | tf_op jit(solution)/shard_map/reshape.7
  30.6 2.6 %fusion.69 = (f32[16,8,24]{2,1,0:T(8,128)S(1)}, f32[16,8,24,24]{2,3,1,0:T(8,128)}) fusion(bf16[24,16,8,72]{3,2,1,0:T(8,128)(2,1)S(1)} %reshape.283, bf16[24,16,8,72]{3,2,1,0:T(8,128)(2,1)S(1)} %reshape.282), kind=kOutput, calls=%fused_computation.81 | convolution fusion | flops 10838039 | bytes 1191936 | tf_op jit(solution)/shard_map/vmap()/sub | solution.py:35
  33.2 2.1 %fusion.37 = bf16[1,24,16,8,72]{4,1,3,2,0:T(8,128)(2,1)S(1)} fusion(f32[16,8,24,24]{2,3,1,0:T(8,128)} %get-tuple-element.20, bf16[24,16,8,72]{3,2,1,0:T(8,128)(2,1)S(1)} %copy-done.3, f32[16,8,24]{2,1,0:T(8,128)S(1)} %get-tuple-element.19), kind=kOutput, calls=%fused_computation.45 | convolution fusion | flops 10985472 | bytes 1191936 | tf_op jit(solution)/shard_map/vmap(bnlm,mbnd->lbnd)/dot_general | solution.py:38
  35.4 0.2 copy.39
  35.5 0.6 convert_element_type.127
  36.1 10.9 %all_to_all.39 = bf16[1,24,16,576]{3,2,0,1:T(8,128)(2,1)S(1)} all-to-all(bf16[1,24,16,576]{3,2,0,1:T(8,128)(2,1)S(1)} %bitcast.90), channel_id=1, replica_groups=mesh['frame'=8,'height'=4] {'height'}, dimensions={1} | all-to-all | bytes 884736 | tf_op jit(solution)/shard_map/all_to_all | solution.py:65
  47.0 2.3 %fusion.10 = bf16[1,6,64,1152]{3,2,1,0:T(8,128)(2,1)S(1)} fusion(bf16[6,64,576]{2,1,0:T(8,128)(2,1)S(1)} %bitcast.96, bf16[1,6,64,1152]{3,2,1,0:T(8,128)(2,1)S(1)} %copy-done.2, bf16[2,576,1152]{2,1,0:T(8,128)(2,1)} %param.5), kind=kOutput, calls=%fused_computation.12 | convolution fusion | flops 510935040 | bytes 3538944 | tf_op jit(solution)/shard_map/dot_general | solution.py:43
  49.3 28.1 %all_to_all.40 = bf16[1,8,48,1152]{3,2,0,1:T(8,128)(2,1)S(1)} all-to-all(bf16[1,8,48,1152]{3,2,0,1:T(8,128)(2,1)S(1)} %bitcast.92), channel_id=1, replica_groups=mesh['frame'=8,'height'=4] {'frame'}, dimensions={1} | all-to-all | bytes 1769472 | tf_op jit(solution)/shard_map/all_to_all | solution.py:71
  77.5 0.2 convert_reduce_fusion
  77.7 0.4 fusion.22
  78.1 0.3 fusion.19
  78.4 4.5 %fusion.15 = bf16[384,1728]{0,1:T(8,128)(2,1)S(1)} fusion(bf16[384,1152]{1,0:T(8,128)(2,1)S(1)} %bitcast.93, bf16[2,1152,1728]{1,2,0:T(8,128)(2,1)} %param.4), kind=kOutput, calls=%fused_computation.15 | convolution fusion | flops 1529487360 | bytes 6193152 | tf_op jit(solution)/shard_map/dot_general | solution.py:19
  82.8 1.8 %copy.43 = bf16[384,1728]{1,0:T(8,128)(2,1)S(1)} copy(bf16[384,1728]{0,1:T(8,128)(2,1)S(1)} %fusion.15) | data formatting | bytes 2654208 | tf_op jit(solution)/shard_map/convert_element_type | solution.py:20
  84.6 0.3 fusion.67
  84.9 0.8 reshape.287
  85.7 0.8 reshape.288
  86.5 1.7 %reshape.286 = bf16[8,48,8,72]{3,2,1,0:T(8,128)(2,1)} reshape(bf16[8,48,576]{2,1,0:T(8,128)(2,1)S(1)} %get-tuple-element.13) | data formatting | bytes 884736 | tf_op jit(solution)/shard_map/reshape | solution.py:31
  88.1 2.8 %fusion.74 = (f32[48,8,8]{2,1,0:T(8,128)S(1)}, f32[48,8,8,8]{2,3,1,0:T(8,128)}) fusion(bf16[8,48,8,72]{3,2,1,0:T(8,128)(2,1)S(1)} %reshape.288, bf16[8,48,8,72]{3,2,1,0:T(8,128)(2,1)S(1)} %reshape.287), kind=kOutput, calls=%fused_computation.82 | convolution fusion | flops 3612679 | bytes 995328 | tf_op jit(solution)/shard_map/sub | solution.py:35
  90.9 2.2 %fusion.38 = bf16[8,48,8,72]{3,0,2,1:T(8,128)(2,1)S(1)} fusion(f32[48,8,8,8]{2,3,1,0:T(8,128)} %get-tuple-element.22, bf16[8,48,8,72]{3,2,1,0:T(8,128)(2,1)S(1)} %copy-done.4, f32[48,8,8]{2,1,0:T(8,128)S(1)} %get-tuple-element.21), kind=kOutput, calls=%fused_computation.46 | convolution fusion | flops 3809280 | bytes 995328 | tf_op jit(solution)/shard_map/bnlm,mbnd->lbnd/dot_general | solution.py:38
  93.1 4.6 %slice_reduce_fusion = (bf16[48,8,72]{2,1,0:T(8,128)(2,1)S(1)}, bf16[48,8,72]{2,1,0:T(8,128)(2,1)S(1)}, bf16[48,8,72]{2,1,0:T(8,128)(2,1)S(1)}, bf16[48,8,72]{2,...) fusion(bf16[8,48,8,72]{3,0,2,1:T(8,128)(2,1)S(1)} %fusion.38), kind=kLoop, calls=%fused_computation.55 | loop fusion | bytes 884736 | tf_op jit(solution)/shard_map/split | solution.py:74
  98.9 16.4 %all_to_all.41 = bf16[8,1,1,48,576]{4,3,2,1,0:T(8,128)(2,1)S(1)} all-to-all(bf16[8,1,1,48,576]{4,3,2,1,0:T(8,128)(2,1)S(1)} %constant_dynamic-update-slice_fusion), channel_id=1, replica_groups=mesh['frame'=8,'height'=4] {'frame'}, dimensions={0} | all-to-all | bytes 884736 | tf_op jit(solution)/shard_map/all_to_all | solution.py:75
  115.3 3.2 %fusion.11 = bf16[1,6,64,1152]{3,2,1,0:T(8,128)(2,1)} fusion(bf16[6,64,576]{2,1,0:T(8,128)(2,1)S(1)} %bitcast.95, bf16[1,6,64,1152]{3,2,1,0:T(8,128)(2,1)S(1)} %copy-done.1, bf16[2,576,1152]{2,1,0:T(8,128)(2,1)} %param.5), kind=kOutput, calls=%fused_computation.13 | convolution fusion | flops 510935040 | bytes 3538944 | tf_op jit(solution)/shard_map/dot_general | solution.py:43
  (35 shorter events, 1.4 us)
Async XLA Ops:
  1.7 21.2 %copy-start.5 = (bf16[2,1152,1728]{1,2,0:T(8,128)(2,1)S(1)}, bf16[2,1152,1728]{1,2,0:T(8,128)(2,1)}, u32[]{:S(2)}) copy-start(bf16[2,1152,1728]{1,2,0:T(8,128)(2,1)} %param.4) | copy-start | bytes 23887876
  30.6 2.6 %copy-start.3 = (bf16[24,16,8,72]{3,2,1,0:T(8,128)(2,1)S(1)}, bf16[24,16,8,72]{3,2,1,0:T(8,128)(2,1)}, u32[]{:S(2)}) copy-start(bf16[24,16,8,72]{3,2,1,0:T(8,128)(2,1)} %reshape.281) | copy-start | bytes 1327108
  35.5 11.5 %copy-start.2 = (bf16[1,6,64,1152]{3,2,1,0:T(8,128)(2,1)S(1)}, bf16[1,6,64,1152]{3,2,1,0:T(8,128)(2,1)}, u32[]{:S(2)}) copy-start(bf16[1,6,64,1152]{3,2,1,0:T(8,128)(2,1)} %param.3) | copy-start | bytes 2654212
  49.3 28.7 %copy-start = (bf16[1,6,64,1152]{3,2,1,0:T(8,128)(2,1)}, bf16[1,6,64,1152]{3,2,1,0:T(8,128)(2,1)S(1)}, u32[]{:S(2)}) copy-start(bf16[1,6,64,1152]{3,2,1,0:T(8,128)(2,1)S(1)} %fusion.10) | copy-start | bytes 2654212
  88.1 2.8 %copy-start.4 = (bf16[8,48,8,72]{3,2,1,0:T(8,128)(2,1)S(1)}, bf16[8,48,8,72]{3,2,1,0:T(8,128)(2,1)}, u32[]{:S(2)}) copy-start(bf16[8,48,8,72]{3,2,1,0:T(8,128)(2,1)} %reshape.286) | copy-start | bytes 1327108
  97.7 17.6 %copy-start.1 = (bf16[1,6,64,1152]{3,2,1,0:T(8,128)(2,1)S(1)}, bf16[1,6,64,1152]{3,2,1,0:T(8,128)(2,1)}, u32[]{:S(2)}) copy-start(bf16[1,6,64,1152]{3,2,1,0:T(8,128)(2,1)} %copy-done) | copy-start | bytes 2654212
